TPU v7x, 32 devices: a whole 2x2x4 slice. The times are simulated.
32 devices in a mesh: trc: 4 (over z), lat: 4 (over x, core), lon: 2 (over y).
Axes of the slice: x: 2, y: 2, z: 4, core: 2. Of those that a mesh axis runs over, the one named last changes fastest.
Arguments:
- species_concentrations: float32 [32, 8, 128, 256], P('trc', None, 'lat', 'lon'), may hold values from 0.2 to 4
- zonal_velocity_array: float32 [8, 128, 256], P('trc', 'lat', 'lon'), may hold values from -2.5 to 2.5
- meridional_velocity_array: float32 [8, 128, 256], P('trc', 'lat', 'lon'), may hold values from -2.5 to 2.5
- thermal_anomaly: float32 [8, 128, 256], P('trc', 'lat', 'lon'), may hold values from -6 to 6
- ocean_top_height_grid: float32 [128, 256], P('lat', 'lon'), may hold values from -6 to 6
- water_layer_tally: int32 [128, 256], P('lat', 'lon'), may hold values from 0 to 8
- species_interaction_table: float32 [32, 32], replicated, may hold values from -1 to 1
- species_production_pace: float32 [32], replicated, may hold values from 0.2 to 2
- photon_uptake: float32 [32], replicated, may hold values from 0.01 to 0.1
Outputs:
- updated_tracers: float32 [32, 8, 128, 256], P('trc', None, 'lat', 'lon')
- east_out: float32 [8, 128, 256], P('trc', 'lat', 'lon')
- north_out: float32 [8, 128, 256], P('trc', 'lat', 'lon')
- temperature_out: float32 [8, 128, 256], P('trc', 'lat', 'lon')
- height_out: float32 [128, 256], P('lat', 'lon')
Inputs may be any that keep to these rules, and one draw needn't show every extreme that they name: `water_layer_tally`: the number of wet levels of a column, counted from the surface; cells below it, and whole columns with 0, are land.
All inputs are finite; a program needn't handle non-finite values.
Results may differ from a plain program's by a relative error of at most 0.0003.
Values sent between devices are 32-bit elements; how exact they have to be, the bound alone decides.
No kernel may reach another device: no remote copies, remote signals or barrier semaphores. Data moves between devices by JAX's collectives and lax.ppermute only.
A program may use at most 64 MiB of HBM per device.

v0:
```python
import math
import jax
import jax.numpy as jnp
from jax import lax
from jax.sharding import PartitionSpec as P

HIGHEST = lax.Precision.HIGHEST
TIME_STEP = 0.1
GRAVITY = 1.0
VISCOSITY = 0.2
BOTTOM_DRAG = 0.05
DEPTH_SCALE = 0.5
CORIOLIS_SCALE = 0.5
COLUMN_DEPTH = 2.0
WATER_ABSORB = 0.2
HALF_LIGHT = 0.5
REACT_STEP = 0.1
WARMING_WEIGHT = 1.0


def padded(block, sides, width, periodic):
    for axis, dim in sides:
        count = lax.axis_size(axis)
        forward = [(i, i + 1) for i in range(count - 1)]
        if periodic:
            forward.append((count - 1, 0))
        backward = [(target, source) for source, target in forward]
        low = lax.ppermute(
            lax.slice_in_dim(block, block.shape[dim] - width, None, axis=dim), axis, forward
        )
        high = lax.ppermute(lax.slice_in_dim(block, 0, width, axis=dim), axis, backward)
        block = jnp.concatenate([low, block, high], axis=dim)
    return block


def limited_slope(ahead, behind):
    smaller = jnp.minimum(jnp.abs(ahead), jnp.abs(behind))
    return jnp.where(
        ahead * behind > 0, jnp.where(ahead > 0, smaller, -smaller), jnp.zeros_like(smaller)
    )


def face_flux(before, center, after, beyond, vel_here, vel_next, wet_here, wet_next):
    courant = 0.5 * (vel_here + vel_next) * wet_here * wet_next
    upwind_pos = center + 0.5 * (1.0 - courant) * limited_slope(after - center, center - before)
    upwind_neg = after - 0.5 * (1.0 + courant) * limited_slope(beyond - after, after - center)
    return courant * jnp.where(courant >= 0, upwind_pos, upwind_neg)


def transport(field, flow_east, flow_north, wet):
    free_top_height, width = (field.shape[-2], field.shape[-1])
    rows = slice(2, free_top_height - 2)
    cols = slice(2, width - 2)
    flux_x = face_flux(
        field[..., rows, 0 : width - 3],
        field[..., rows, 1 : width - 2],
        field[..., rows, 2 : width - 1],
        field[..., rows, 3:width],
        flow_east[..., rows, 1 : width - 2],
        flow_east[..., rows, 2 : width - 1],
        wet[..., rows, 1 : width - 2],
        wet[..., rows, 2 : width - 1],
    )
    flux_y = face_flux(
        field[..., 0 : free_top_height - 3, cols],
        field[..., 1 : free_top_height - 2, cols],
        field[..., 2 : free_top_height - 1, cols],
        field[..., 3:free_top_height, cols],
        flow_north[..., 1 : free_top_height - 2, cols],
        flow_north[..., 2 : free_top_height - 1, cols],
        wet[..., 1 : free_top_height - 2, cols],
        wet[..., 2 : free_top_height - 1, cols],
    )
    return (
        field[..., rows, cols]
        - (flux_x[..., 1:] - flux_x[..., :-1])
        - (flux_y[..., 1:, :] - flux_y[..., :-1, :])
    )


def ocean_core(stacked, north, south, east, west, wet, coriolis):
    count = (stacked.shape[0] - 1) // 2
    zonal_flow_value = stacked[:count]
    meridional_flow_value = stacked[count : 2 * count]
    free_top_height = stacked[2 * count]
    lap_east = north[:count] + south[:count] + east[:count] + west[:count] - 4.0 * zonal_flow_value
    lap_north = (
        north[count : 2 * count]
        + south[count : 2 * count]
        + east[count : 2 * count]
        + west[count : 2 * count]
        - 4.0 * meridional_flow_value
    )
    grad_x = 0.5 * (east[2 * count] - west[2 * count])
    grad_y = 0.5 * (north[2 * count] - south[2 * count])
    div_levels = 0.5 * (east[:count] - west[:count]) + 0.5 * (
        north[count : 2 * count] - south[count : 2 * count]
    )
    new_east = wet * (
        zonal_flow_value
        + TIME_STEP
        * (
            coriolis * meridional_flow_value
            - GRAVITY * grad_x
            + VISCOSITY * lap_east
            - BOTTOM_DRAG * zonal_flow_value
        )
    )
    new_north = wet * (
        meridional_flow_value
        + TIME_STEP
        * (
            -coriolis * zonal_flow_value
            - GRAVITY * grad_y
            + VISCOSITY * lap_north
            - BOTTOM_DRAG * meridional_flow_value
        )
    )
    return (new_east, new_north, free_top_height, jnp.sum(div_levels, 0))


def ocean_step(zonal_flow_value, meridional_flow_value, free_top_height, wet, coriolis):
    stacked = jnp.concatenate([zonal_flow_value, meridional_flow_value, free_top_height[None]], 0)
    by_lat = padded(stacked, (("lat", 1),), 1, False)
    by_lon = padded(stacked, (("lon", 2),), 1, True)
    new_east, new_north, free_top_height, partial_div = ocean_core(
        stacked,
        by_lat[:, 2:, :],
        by_lat[:, :-2, :],
        by_lon[:, :, 2:],
        by_lon[:, :, :-2],
        wet,
        coriolis,
    )
    divergence = lax.psum(partial_div, "trc")
    return (new_east, new_north, free_top_height - TIME_STEP * DEPTH_SCALE * divergence)


def widen_flow(flow, width):
    rows_ext = padded(flow, (("lat", 2),), width, False)
    return padded(rows_ext, (("lon", 3),), width, True)


def widen_tracers(field, width):
    rows_ext = padded(field, (("lat", 2),), width, False)
    return padded(rows_ext, (("lon", 3),), width, True)


def light_profile(absorbed, wet, surface):
    levels = absorbed.shape[0]
    layer = COLUMN_DEPTH / levels * (WATER_ABSORB + absorbed) * wet
    above = jnp.cumsum(layer, 0) - layer
    top_light = surface[None, :, None] * jnp.exp(-above)
    return (top_light * (1.0 - jnp.exp(-layer)), top_light / (top_light + HALF_LIGHT))


def body(
    species_concentrations,
    zonal_velocity_array,
    meridional_velocity_array,
    thermal_anomaly,
    ocean_top_height_grid,
    water_layer_tally,
    species_interaction_table,
    species_production_pace,
    photon_uptake,
):
    tracer_count, levels, lat_rows, lon_cols = species_concentrations.shape
    own_levels = zonal_velocity_array.shape[0]
    trc_place = lax.axis_index("trc")
    lat_total = lat_rows * lax.axis_size("lat")
    lat_global = (lax.axis_index("lat") * lat_rows + jnp.arange(lat_rows)).astype(jnp.float32)
    angle = math.pi * ((lat_global + 0.5) / lat_total - 0.5)
    coriolis = CORIOLIS_SCALE * jnp.sin(angle)[:, None]
    surface = 1.0 + jnp.cos(angle)
    depth_index = jnp.arange(levels)
    wet_all = (depth_index[:, None, None] < water_layer_tally[None]).astype(jnp.float32)
    wet_own = lax.dynamic_slice_in_dim(wet_all, trc_place * own_levels, own_levels, 0)
    east_start = wet_own * zonal_velocity_array
    north_start = wet_own * meridional_velocity_array
    zonal_flow_value, meridional_flow_value, free_top_height = (
        east_start,
        north_start,
        ocean_top_height_grid,
    )
    for substep in range(2):
        zonal_flow_value, meridional_flow_value, free_top_height = ocean_step(
            zonal_flow_value, meridional_flow_value, free_top_height, wet_own, coriolis
        )
    velocity = lax.all_gather(jnp.stack([east_start, north_start]), "trc", axis=1, tiled=True)
    flow = jnp.concatenate([velocity, wet_all[None]], 0)
    flow_ext = widen_flow(flow, 4)
    first = transport(
        widen_tracers(species_concentrations, 4), flow_ext[0], flow_ext[1], flow_ext[2]
    )
    inner = flow_ext[:, :, 2:-2, 2:-2]
    moved = transport(first, inner[0], inner[1], inner[2])
    share = lat_rows // lax.axis_size("trc")
    columns = lax.all_to_all(moved, "trc", split_axis=2, concat_axis=0, tiled=True)
    wet_cols = lax.dynamic_slice_in_dim(wet_all, trc_place * share, share, 1)
    surface_cols = lax.dynamic_slice_in_dim(surface, trc_place * share, share, 0)
    absorbed = jnp.einsum("n,nkyx->kyx", photon_uptake, jnp.abs(columns), precision=HIGHEST)
    solar_warming, light_factor = light_profile(absorbed, wet_cols, surface_cols)
    mixed = jnp.einsum("mn,nkyx->mkyx", species_interaction_table, columns, precision=HIGHEST)
    species_postchemistry = columns + wet_cols * REACT_STEP * (
        mixed + species_production_pace[:, None, None, None] * light_factor * columns
    )
    updated_tracers = lax.all_to_all(
        species_postchemistry, "trc", split_axis=0, concat_axis=2, tiled=True
    )
    pointwise_warming_pace = lax.all_to_all(
        solar_warming, "trc", split_axis=0, concat_axis=1, tiled=True
    )
    return (
        updated_tracers,
        zonal_flow_value,
        meridional_flow_value,
        thermal_anomaly + WARMING_WEIGHT * pointwise_warming_pace,
        free_top_height,
    )


def solution(mesh):
    return jax.shard_map(
        body,
        mesh=mesh,
        in_specs=(
            P("trc", None, "lat", "lon"),
            P("trc", "lat", "lon"),
            P("trc", "lat", "lon"),
            P("trc", "lat", "lon"),
            P("lat", "lon"),
            P("lat", "lon"),
            P(),
            P(),
            P(),
        ),
        out_specs=(
            P("trc", None, "lat", "lon"),
            P("trc", "lat", "lon"),
            P("trc", "lat", "lon"),
            P("trc", "lat", "lon"),
            P("lat", "lon"),
        ),
        check_vma=False,
    )
```

profile of v0, /device:TPU:0, one launch (start us, length us, event | category | flops | bytes accessed | tf_op | source)
XLA Modules:
  0.0 207.8 jit_solution(16878511505992361957)
XLA Ops:
  3.0 15.7 %all_gather.3 = f32[2,8,32,128]{3,2,0,1:T(8,128)S(1)} all-gather(f32[2,2,32,128]{3,2,0,1:T(8,128)S(1)} %pad_maximum_fusion.8), channel_id=1, replica_groups=mesh['trc'=4,'lat'=4,'lon'=2] {'trc'}, dimensions={1}, use_global_device_ids=true | all-gather | bytes 327680 | tf_op jit(solution)/shard_map/all_gather | solution.py:190
  18.9 1.3 collective-permute-start.5
  20.2 3.0 %collective-permute-start.4 = (f32[3,8,4,128]{3,1,2,0:T(8,128)S(1)}, f32[3,8,4,128]{3,1,2,0:T(8,128)S(1)}, u32[]{:S(2)}, u32[]{:S(2)}) collective-permute-start(f32[3,8,4,128]{3,1,2,0:T(8,128)S(1)} %get-tuple-element.30), channel_id=1, source_target_pairs={{0,2},{2,4},{4,6},{1,3},{3,5},{5,7},{8,10},{10,12},{12,14},{9,11},... | collective-permute-start | bytes 147464 | tf_op jit(solution)/shard_map/ppermute | solution.py:28
  25.0 1.5 collective-permute-start.7
  27.8 1.3 collective-permute-start.1
  29.7 4.0 %collective-permute-start = (f32[8,8,4,128]{3,1,2,0:T(8,128)}, f32[8,8,4,128]{3,1,2,0:T(8,128)}, u32[]{:S(2)}, u32[]{:S(2)}) collective-permute-start(f32[8,8,4,128]{3,1,2,0:T(8,128)} %copy.159), channel_id=1, source_target_pairs={{0,2},{2,4},{4,6},{1,3},{3,5},{5,7},{8,10},{10,12},{12,14},{9,11},... | collective-permute-start | bytes 393224 | tf_op jit(solution)/shard_map/ppermute | solution.py:28
  33.7 2.7 %copy.131 = f32[8,8,32,128]{2,1,3,0:T(8,128)} copy(f32[8,8,32,128]{3,2,1,0:T(8,128)S(1)} %copy-done.8) | data formatting | bytes 2097152 | tf_op args[0]
  36.4 2.5 %collective-permute-done.7 = f32[3,8,40,4]{3,1,2,0:T(8,128)S(1)} collective-permute-done((f32[3,8,40,4]{3,1,2,0:T(8,128)}, f32[3,8,40,4]{3,1,2,0:T(8,128)S(1)}, u32[]{:S(2)}, u32[]{:S(2)}) %collective-permute-start.7) | collective-permute-done | bytes 15392 | tf_op jit(solution)/shard_map/ppermute | solution.py:31
  38.9 10.5 %collective-permute-done.6 = f32[3,8,40,4]{3,1,2,0:T(8,128)S(1)} collective-permute-done((f32[3,8,40,4]{3,1,2,0:T(8,128)S(1)}, f32[3,8,40,4]{3,1,2,0:T(8,128)S(1)}, u32[]{:S(2)}, u32[]{:S(2)}) %collective-permute-start.6) | collective-permute-done | bytes 15392 | tf_op jit(solution)/shard_map/ppermute | solution.py:28
  55.2 3.6 %copy.132 = f32[8,8,4,128]{2,1,3,0:T(8,128)} copy(f32[8,8,4,128]{3,1,2,0:T(8,128)} %collective-permute-done.1) | data formatting | bytes 262144 | tf_op jit(solution)/shard_map/ppermute | solution.py:31
  58.8 3.5 %copy.130 = f32[8,8,4,128]{2,1,3,0:T(8,128)} copy(f32[8,8,4,128]{3,1,2,0:T(8,128)} %collective-permute-done) | data formatting | bytes 262144 | tf_op jit(solution)/shard_map/ppermute | solution.py:28
  62.3 2.1 %pad_maximum_fusion.5 = (f32[8,8,40,4]{2,1,3,0:T(8,128)}, f32[8,8,40,4]{2,1,3,0:T(8,128)}) fusion(f32[8,8,4,128]{2,1,3,0:T(8,128)} %copy.132, f32[8,8,32,128]{2,1,3,0:T(8,128)} %copy.131, f32[8,8,4,128]{2,1,3,0:T(8,128)} %copy.130), kind=kLoop, calls=%fused_computation.120 | loop fusion | flops 40960 | bytes 1392640 | tf_op jit(solution)/shard_map/slice | solution.py:29
  64.4 1.5 collective-permute-start.3
  69.0 1.2 copy.143
  70.6 1.2 copy.141
  72.3 1.4 copy.138
  73.6 1.4 copy.137
  75.0 1.3 copy.136
  76.3 1.9 copy.150
  80.4 2.1 %copy.146 = f32[8,32,129]{1,0,2:T(8,128)} copy(f32[8,32,129]{2,0,1:T(8,128)} %get-tuple-element.37) | data formatting | bytes 264192 | tf_op jit(solution)/shard_map/mul | solution.py:46
  82.5 2.1 %copy.145 = f32[8,32,129]{1,0,2:T(8,128)} copy(f32[8,32,129]{2,0,1:T(8,128)} %get-tuple-element.36) | data formatting | bytes 264192 | tf_op jit(solution)/shard_map/mul | solution.py:45
  84.6 1.2 copy.144
  85.9 6.0 %pad_maximum_fusion = f32[8,8,40,136]{2,1,3,0:T(8,128)S(1)} fusion(f32[8,8,40,4]{2,1,3,0:T(8,128)} %collective-permute-done.3, f32[8,8,4,128]{2,1,3,0:T(8,128)} %copy.132, f32[8,8,32,128]{2,1,3,0:T(8,128)} %copy.131, f32[8,8,4,128]{2,1,3,0:T(8,128)} %copy.130, f32[8,8,40,4]{2,1,3,0:T(8,128)} %collective-permute-done.2), kind=kLoop, calls=%fused_computation.8 | loop fusion | flops 1392640 | bytes 2785280 | tf_op jit(solution)/shard_map/concatenate | solution.py:32
  91.8 4.3 %fusion.12 = f32[8,8,37,132]{2,1,3,0:T(8,128)S(1)} fusion(f32[8,8,40,136]{2,1,3,0:T(8,128)S(1)} %pad_maximum_fusion, f32[8,37,132]{1,0,2:T(8,128)S(1)} %copy.142, f32[8,37,132]{1,0,2:T(8,128)S(1)} %copy-done.1, f32[8,37,132]{1,0,2:T(8,128)S(1)} %copy.139, pred[8,37,132]{1,0,2:T(8,128)(4,1)S(1)} %copy.140), kind=kLoop, calls=%fused_computation.26 | loop fusion | flops 8126976 | bytes 6759456 | tf_op jit(solution)/shard_map/mul | solution.py:47
  96.1 5.1 %fusion.4 = f32[8,8,36,133]{2,1,3,0:T(8,128)S(1)} fusion(f32[8,8,40,136]{2,1,3,0:T(8,128)S(1)} %pad_maximum_fusion, f32[8,36,133]{1,0,2:T(8,128)S(1)} %copy.138, f32[8,36,133]{1,0,2:T(8,128)S(1)} %copy.137, f32[8,36,133]{1,0,2:T(8,128)S(1)} %copy.135, pred[8,36,133]{1,0,2:T(8,128)(4,1)S(1)} %copy.136), kind=kLoop, calls=%fused_computation.13 | loop fusion | flops 7967232 | bytes 6626592 | tf_op jit(solution)/shard_map/mul | solution.py:47
  101.3 2.6 %fusion.16 = f32[8,8,36,132]{2,1,3,0:T(8,128)S(1)} fusion(f32[8,8,37,132]{2,1,3,0:T(8,128)S(1)} %fusion.12, f32[8,8,36,133]{2,1,3,0:T(8,128)S(1)} %fusion.4, f32[8,8,40,136]{2,1,3,0:T(8,128)S(1)} %pad_maximum_fusion), kind=kLoop, calls=%fused_computation.31 | loop fusion | flops 1216512 | bytes 7299072 | tf_op jit(solution)/shard_map/sub | solution.py:75
  103.9 4.2 %fusion.30 = f32[8,8,33,128]{2,1,3,0:T(8,128)S(1)} fusion(f32[8,8,36,132]{2,1,3,0:T(8,128)S(1)} %fusion.16, f32[8,33,128]{1,0,2:T(8,128)S(1)} %copy-done.6, f32[8,33,128]{1,0,2:T(8,128)S(1)} %copy-done.7, f32[8,33,128]{1,0,2:T(8,128)S(1)} %copy-done.5, pred[8,33,128]{1,0,2:T(8,128)(4,1)S(1)} %copy.148), kind=kLoop, calls=%fused_computation.56 | loop fusion | flops 7028736 | bytes 5846016 | tf_op jit(solution)/shard_map/mul | solution.py:47
  108.1 4.7 %fusion.22 = f32[8,8,32,129]{2,1,3,0:T(8,128)S(1)} fusion(f32[8,8,36,132]{2,1,3,0:T(8,128)S(1)} %fusion.16, f32[8,32,129]{1,0,2:T(8,128)S(1)} %copy-done.3, f32[8,32,129]{1,0,2:T(8,128)S(1)} %copy-done.4, f32[8,32,129]{1,0,2:T(8,128)S(1)} %copy-done.2, pred[8,32,129]{1,0,2:T(8,128)(4,1)S(1)} %copy.144), kind=kLoop, calls=%fused_computation.43 | loop fusion | flops 6868992 | bytes 5713152 | tf_op jit(solution)/shard_map/mul | solution.py:47
  112.9 3.8 %fusion.34 = f32[8,8,32,128]{2,1,3,0:T(8,128)} fusion(f32[8,8,33,128]{2,1,3,0:T(8,128)S(1)} %fusion.30, f32[8,8,32,129]{2,1,3,0:T(8,128)S(1)} %fusion.22, f32[8,8,36,132]{2,1,3,0:T(8,128)S(1)} %fusion.16), kind=kLoop, calls=%fused_computation.61 | loop fusion | flops 1048576 | bytes 6291456 | tf_op jit(solution)/shard_map/sub | solution.py:75
  116.6 3.9 %copy.151 = f32[8,8,32,128]{3,1,0,2:T(8,128)} copy(f32[8,8,32,128]{2,1,3,0:T(8,128)} %fusion.34) | data formatting | bytes 2097152 | tf_op jit(solution)/shard_map/sub | solution.py:75
  120.6 5.2 %all-to-all-start = ((f32[8,8,32,128]{3,1,0,2:T(8,128)}), f32[8,8,32,128]{3,1,0,2:T(8,128)S(1)}, u32[]{:S(2)}, u32[]{:S(2)}) async-start(f32[8,8,32,128]{3,1,0,2:T(8,128)} %copy.151), calls=%async_computation | async-start | bytes 2097152 | tf_op jit(solution)/shard_map/all_to_all | solution.py:199
  125.8 1.3 collective-permute-start.11
  127.1 1.3 collective-permute-start.10
  128.5 1.6 collective-permute-start.9
  130.8 2.2 %collective-permute-done.9 = f32[5,32,1]{2,1,0:T(8,128)S(1)} collective-permute-done((f32[5,32,1]{2,1,0:T(8,128)S(1)}, f32[5,32,1]{2,1,0:T(8,128)S(1)}, u32[]{:S(2)}, u32[]{:S(2)}) %collective-permute-start.9) | collective-permute-done | bytes 672 | tf_op jit(solution)/shard_map/ppermute | solution.py:28
  133.0 2.2 %collective-permute-done.8 = f32[5,32,1]{2,1,0:T(8,128)S(1)} collective-permute-done((f32[5,32,1]{2,1,0:T(8,128)S(1)}, f32[5,32,1]{2,1,0:T(8,128)S(1)}, u32[]{:S(2)}, u32[]{:S(2)}) %collective-permute-start.8) | collective-permute-done | bytes 672 | tf_op jit(solution)/shard_map/ppermute | solution.py:31
  135.4 24.5 %psum.14 = f32[32,128]{1,0:T(8,128)S(1)} all-reduce(f32[32,128]{1,0:T(8,128)S(1)} %multiply_reduce_fusion.1), channel_id=1, replica_groups=mesh['trc'=4,'lat'=4,'lon'=2] {'trc'}, use_global_device_ids=true, to_apply=%region_2.0 | all-reduce | flops 4096 | bytes 32768 | tf_op jit(solution)/shard_map/psum | solution.py:135
  161.7 3.4 %all-to-all-start.2 = ((f32[8,8,128]{2,1,0:T(8,128)}), f32[8,8,128]{2,1,0:T(8,128)S(1)}, u32[]{:S(2)}, u32[]{:S(2)}) async-start(f32[8,8,128]{2,1,0:T(8,128)} %get-tuple-element.40), calls=%async_computation.2 | async-start | bytes 65536 | tf_op jit(solution)/shard_map/all_to_all | solution.py:211
  165.1 1.3 fusion.38
  166.4 1.6 copy.153
  168.0 2.7 %all-to-all-done.2 = f32[8,8,128]{2,1,0:T(8,128)S(1)} async-done(((f32[8,8,128]{2,1,0:T(8,128)}), f32[8,8,128]{2,1,0:T(8,128)S(1)}, u32[]{:S(2)}, u32[]{:S(2)}) %all-to-all-start.2) | async-done | bytes 32800 | tf_op jit(solution)/shard_map/all_to_all | solution.py:211
  170.7 3.5 %all-to-all-start.1 = ((f32[32,8,8,128]{3,2,1,0:T(8,128)}), f32[32,8,8,128]{3,2,1,0:T(8,128)S(1)}, u32[]{:S(2)}, u32[]{:S(2)}) async-start(f32[32,8,8,128]{3,2,1,0:T(8,128)} %copy.153), calls=%async_computation.1 | async-start | bytes 2097152 | tf_op jit(solution)/shard_map/all_to_all | solution.py:208
  174.3 1.3 collective-permute-start.15
  175.6 1.3 collective-permute-start.14
  177.0 1.6 collective-permute-start.13
  179.1 3.1 %collective-permute-done.13 = f32[5,32,1]{2,1,0:T(8,128)S(1)} collective-permute-done((f32[5,32,1]{2,1,0:T(8,128)S(1)}, f32[5,32,1]{2,1,0:T(8,128)S(1)}, u32[]{:S(2)}, u32[]{:S(2)}) %collective-permute-start.13) | collective-permute-done | bytes 672 | tf_op jit(solution)/shard_map/ppermute | solution.py:28
  182.2 1.8 collective-permute-done.12
  184.1 19.9 %psum.15 = f32[32,128]{1,0:T(8,128)S(1)} all-reduce(f32[32,128]{1,0:T(8,128)S(1)} %multiply_reduce_fusion), channel_id=1, replica_groups=mesh['trc'=4,'lat'=4,'lon'=2] {'trc'}, use_global_device_ids=true, to_apply=%region_4.5 | all-reduce | flops 4096 | bytes 32768 | tf_op jit(solution)/shard_map/psum | solution.py:135
  (96 shorter events, 25.3 us)
Async XLA Ops:
  0.6 164.5 %copy-start = (f32[32,32]{1,0:T(8,128)S(1)}, f32[32,32]{1,0:T(8,128)}, u32[]{:S(2)}) copy-start(f32[32,32]{1,0:T(8,128)} %param.15) | copy-start | bytes 12292
  0.6 26.4 %copy-start.8 = (f32[8,8,32,128]{3,2,1,0:T(8,128)S(1)}, f32[8,8,32,128]{3,2,1,0:T(8,128)}, u32[]{:S(2)}) copy-start(f32[8,8,32,128]{3,2,1,0:T(8,128)} %param.9) | copy-start | bytes 3145732
  18.9 4.3 %collective-permute-start.5 = (f32[3,8,4,128]{3,1,2,0:T(8,128)S(1)}, f32[3,8,4,128]{3,1,2,0:T(8,128)S(1)}, u32[]{:S(2)}, u32[]{:S(2)}) collective-permute-start(f32[3,8,4,128]{3,1,2,0:T(8,128)S(1)} %get-tuple-element.31), channel_id=1, source_target_pairs={{2,0},{4,2},{6,4},{3,1},{5,3},{7,5},{10,8},{12,10},{14,12},{11,9},... | collective-permute-start | bytes 147464 | tf_op jit(solution)/shard_map/ppermute | solution.py:31
  20.2 3.9 %collective-permute-start.4 = (f32[3,8,4,128]{3,1,2,0:T(8,128)S(1)}, f32[3,8,4,128]{3,1,2,0:T(8,128)S(1)}, u32[]{:S(2)}, u32[]{:S(2)}) collective-permute-start(f32[3,8,4,128]{3,1,2,0:T(8,128)S(1)} %get-tuple-element.30), channel_id=1, source_target_pairs={{0,2},{2,4},{4,6},{1,3},{3,5},{5,7},{8,10},{10,12},{12,14},{9,11},... | collective-permute-start | bytes 147464 | tf_op jit(solution)/shard_map/ppermute | solution.py:28
  25.0 13.9 %collective-permute-start.7 = (f32[3,8,40,4]{3,1,2,0:T(8,128)}, f32[3,8,40,4]{3,1,2,0:T(8,128)S(1)}, u32[]{:S(2)}, u32[]{:S(2)}) collective-permute-start(f32[3,8,40,4]{3,1,2,0:T(8,128)} %get-tuple-element.29), channel_id=1, source_target_pairs={{1,0},{0,1},{3,2},{2,3},{5,4},{4,5},{7,6},{6,7},{9,8},{8,9},{11,10... | collective-permute-start | bytes 46088 | tf_op jit(solution)/shard_map/ppermute | solution.py:31
  26.5 22.9 %collective-permute-start.6 = (f32[3,8,40,4]{3,1,2,0:T(8,128)S(1)}, f32[3,8,40,4]{3,1,2,0:T(8,128)S(1)}, u32[]{:S(2)}, u32[]{:S(2)}) collective-permute-start(f32[3,8,40,4]{3,1,2,0:T(8,128)S(1)} %get-tuple-element.28), channel_id=1, source_target_pairs={{0,1},{1,0},{2,3},{3,2},{4,5},{5,4},{6,7},{7,6},{8,9},{9,8},{10,11... | collective-permute-start | bytes 46088 | tf_op jit(solution)/shard_map/ppermute | solution.py:28
  27.8 27.4 %collective-permute-start.1 = (f32[8,8,4,128]{3,1,2,0:T(8,128)}, f32[8,8,4,128]{3,1,2,0:T(8,128)}, u32[]{:S(2)}, u32[]{:S(2)}) collective-permute-start(f32[8,8,4,128]{3,1,2,0:T(8,128)} %copy.160), channel_id=1, source_target_pairs={{2,0},{4,2},{6,4},{3,1},{5,3},{7,5},{10,8},{12,10},{14,12},{11,9},... | collective-permute-start | bytes 393224 | tf_op jit(solution)/shard_map/ppermute | solution.py:31
  29.7 29.1 %collective-permute-start = (f32[8,8,4,128]{3,1,2,0:T(8,128)}, f32[8,8,4,128]{3,1,2,0:T(8,128)}, u32[]{:S(2)}, u32[]{:S(2)}) collective-permute-start(f32[8,8,4,128]{3,1,2,0:T(8,128)} %copy.159), channel_id=1, source_target_pairs={{0,2},{2,4},{4,6},{1,3},{3,5},{5,7},{8,10},{10,12},{12,14},{9,11},... | collective-permute-start | bytes 393224 | tf_op jit(solution)/shard_map/ppermute | solution.py:28
  64.4 21.4 %collective-permute-start.3 = (f32[8,8,40,4]{2,1,3,0:T(8,128)}, f32[8,8,40,4]{2,1,3,0:T(8,128)}, u32[]{:S(2)}, u32[]{:S(2)}) collective-permute-start(f32[8,8,40,4]{2,1,3,0:T(8,128)} %get-tuple-element.19), channel_id=1, source_target_pairs={{1,0},{0,1},{3,2},{2,3},{5,4},{4,5},{7,6},{6,7},{9,8},{8,9},{11,10... | collective-permute-start | bytes 122888 | tf_op jit(solution)/shard_map/ppermute | solution.py:31
  65.9 19.9 %collective-permute-start.2 = (f32[8,8,40,4]{2,1,3,0:T(8,128)}, f32[8,8,40,4]{2,1,3,0:T(8,128)}, u32[]{:S(2)}, u32[]{:S(2)}) collective-permute-start(f32[8,8,40,4]{2,1,3,0:T(8,128)} %get-tuple-element.18), channel_id=1, source_target_pairs={{0,1},{1,0},{2,3},{3,2},{4,5},{5,4},{6,7},{7,6},{8,9},{9,8},{10,11... | collective-permute-start | bytes 122888 | tf_op jit(solution)/shard_map/ppermute | solution.py:28
  70.2 8.0 %copy-start.10 = (f32[8,33,128]{2,0,1:T(8,128)S(1)}, f32[8,33,128]{2,0,1:T(8,128)}, u32[]{:S(2)}) copy-start(f32[8,33,128]{2,0,1:T(8,128)} %get-tuple-element.38) | copy-start | bytes 405508
  85.8 6.0 %copy-start.1 = (f32[8,37,132]{1,0,2:T(8,128)S(1)}, f32[8,37,132]{1,0,2:T(8,128)}, u32[]{:S(2)}) copy-start(f32[8,37,132]{1,0,2:T(8,128)} %copy.141) | copy-start | bytes 468868
  101.2 2.6 %copy-start.5 = (f32[8,33,128]{1,0,2:T(8,128)S(1)}, f32[8,33,128]{1,0,2:T(8,128)}, u32[]{:S(2)}) copy-start(f32[8,33,128]{1,0,2:T(8,128)} %copy.147) | copy-start | bytes 405508
  101.3 2.6 %copy-start.6 = (f32[8,33,128]{1,0,2:T(8,128)S(1)}, f32[8,33,128]{1,0,2:T(8,128)}, u32[]{:S(2)}) copy-start(f32[8,33,128]{1,0,2:T(8,128)} %copy.150) | copy-start | bytes 405508
  101.3 2.6 %copy-start.7 = (f32[8,33,128]{1,0,2:T(8,128)S(1)}, f32[8,33,128]{1,0,2:T(8,128)}, u32[]{:S(2)}) copy-start(f32[8,33,128]{1,0,2:T(8,128)} %copy.149) | copy-start | bytes 405508
  103.9 4.3 %copy-start.2 = (f32[8,32,129]{1,0,2:T(8,128)S(1)}, f32[8,32,129]{1,0,2:T(8,128)}, u32[]{:S(2)}) copy-start(f32[8,32,129]{1,0,2:T(8,128)} %copy.143) | copy-start | bytes 396292
  103.9 4.3 %copy-start.3 = (f32[8,32,129]{1,0,2:T(8,128)S(1)}, f32[8,32,129]{1,0,2:T(8,128)}, u32[]{:S(2)}) copy-start(f32[8,32,129]{1,0,2:T(8,128)} %copy.146) | copy-start | bytes 396292
  103.9 4.3 %copy-start.4 = (f32[8,32,129]{1,0,2:T(8,128)S(1)}, f32[8,32,129]{1,0,2:T(8,128)}, u32[]{:S(2)}) copy-start(f32[8,32,129]{1,0,2:T(8,128)} %copy.145) | copy-start | bytes 396292
  116.6 9.1 %copy-start.9 = (f32[32,128]{1,0:T(8,128)S(1)}, f32[32,128]{1,0:T(8,128)}, u32[]{:S(2)}) copy-start(f32[32,128]{1,0:T(8,128)} %param.13) | copy-start | bytes 49156
  116.6 43.5 %copy-start.12 = (f32[32]{0:T(128)S(1)}, f32[32]{0:T(128)}, u32[]{:S(2)}) copy-start(f32[32]{0:T(128)} %param.17) | copy-start | bytes 388
  116.6 48.5 %copy-start.13 = (f32[32]{0:T(128)S(1)}, f32[32]{0:T(128)}, u32[]{:S(2)}) copy-start(f32[32]{0:T(128)} %param.16) | copy-start | bytes 388
  120.6 39.6 %all-to-all-start = ((f32[8,8,32,128]{3,1,0,2:T(8,128)}), f32[8,8,32,128]{3,1,0,2:T(8,128)S(1)}, u32[]{:S(2)}, u32[]{:S(2)}) async-start(f32[8,8,32,128]{3,1,0,2:T(8,128)} %copy.151), calls=%async_computation | async-start | bytes 2097152 | tf_op jit(solution)/shard_map/all_to_all | solution.py:199
  125.8 9.5 %collective-permute-start.11 = (f32[5,1,128]{2,1,0:T(1,128)S(1)}, f32[5,1,128]{2,1,0:T(1,128)S(1)}, u32[]{:S(2)}, u32[]{:S(2)}) collective-permute-start(f32[5,1,128]{2,1,0:T(1,128)S(1)} %get-tuple-element.55), channel_id=1, source_target_pairs={{0,2},{2,4},{4,6},{1,3},{3,5},{5,7},{8,10},{10,12},{12,14},{9,11},... | collective-permute-start | bytes 7688 | tf_op jit(solution)/shard_map/ppermute | solution.py:28
  127.1 8.2 %collective-permute-start.10 = (f32[5,1,128]{2,1,0:T(1,128)S(1)}, f32[5,1,128]{2,1,0:T(1,128)S(1)}, u32[]{:S(2)}, u32[]{:S(2)}) collective-permute-start(f32[5,1,128]{2,1,0:T(1,128)S(1)} %get-tuple-element.54), channel_id=1, source_target_pairs={{2,0},{4,2},{6,4},{3,1},{5,3},{7,5},{10,8},{12,10},{14,12},{11,9},... | collective-permute-start | bytes 7688 | tf_op jit(solution)/shard_map/ppermute | solution.py:31
  128.5 4.5 %collective-permute-start.9 = (f32[5,32,1]{2,1,0:T(8,128)S(1)}, f32[5,32,1]{2,1,0:T(8,128)S(1)}, u32[]{:S(2)}, u32[]{:S(2)}) collective-permute-start(f32[5,32,1]{2,1,0:T(8,128)S(1)} %get-tuple-element.53), channel_id=1, source_target_pairs={{0,1},{1,0},{2,3},{3,2},{4,5},{5,4},{6,7},{7,6},{8,9},{9,8},{10,11... | collective-permute-start | bytes 1928 | tf_op jit(solution)/shard_map/ppermute | solution.py:28
  130.1 5.2 %collective-permute-start.8 = (f32[5,32,1]{2,1,0:T(8,128)S(1)}, f32[5,32,1]{2,1,0:T(8,128)S(1)}, u32[]{:S(2)}, u32[]{:S(2)}) collective-permute-start(f32[5,32,1]{2,1,0:T(8,128)S(1)} %get-tuple-element.52), channel_id=1, source_target_pairs={{1,0},{0,1},{3,2},{2,3},{5,4},{4,5},{7,6},{6,7},{9,8},{8,9},{11,10... | collective-permute-start | bytes 1928 | tf_op jit(solution)/shard_map/ppermute | solution.py:31
  161.7 44.4 %copy-start.11 = (f32[2,32,128]{2,1,0:T(8,128)S(1)}, f32[2,32,128]{2,1,0:T(8,128)}, u32[]{:S(2)}) copy-start(f32[2,32,128]{2,1,0:T(8,128)} %param.12) | copy-start | bytes 98308
  161.7 9.0 %all-to-all-start.2 = ((f32[8,8,128]{2,1,0:T(8,128)}), f32[8,8,128]{2,1,0:T(8,128)S(1)}, u32[]{:S(2)}, u32[]{:S(2)}) async-start(f32[8,8,128]{2,1,0:T(8,128)} %get-tuple-element.40), calls=%async_computation.2 | async-start | bytes 65536 | tf_op jit(solution)/shard_map/all_to_all | solution.py:211
  170.7 36.0 %all-to-all-start.1 = ((f32[32,8,8,128]{3,2,1,0:T(8,128)}), f32[32,8,8,128]{3,2,1,0:T(8,128)S(1)}, u32[]{:S(2)}, u32[]{:S(2)}) async-start(f32[32,8,8,128]{3,2,1,0:T(8,128)} %copy.153), calls=%async_computation.1 | async-start | bytes 2097152 | tf_op jit(solution)/shard_map/all_to_all | solution.py:208
  174.3 9.7 %collective-permute-start.15 = (f32[5,1,128]{2,1,0:T(1,128)S(1)}, f32[5,1,128]{2,1,0:T(1,128)S(1)}, u32[]{:S(2)}, u32[]{:S(2)}) collective-permute-start(f32[5,1,128]{2,1,0:T(1,128)S(1)} %get-tuple-element.49), channel_id=1, source_target_pairs={{0,2},{2,4},{4,6},{1,3},{3,5},{5,7},{8,10},{10,12},{12,14},{9,11},... | collective-permute-start | bytes 7688 | tf_op jit(solution)/shard_map/ppermute | solution.py:28
  175.6 8.4 %collective-permute-start.14 = (f32[5,1,128]{2,1,0:T(1,128)S(1)}, f32[5,1,128]{2,1,0:T(1,128)S(1)}, u32[]{:S(2)}, u32[]{:S(2)}) collective-permute-start(f32[5,1,128]{2,1,0:T(1,128)S(1)} %get-tuple-element.48), channel_id=1, source_target_pairs={{2,0},{4,2},{6,4},{3,1},{5,3},{7,5},{10,8},{12,10},{14,12},{11,9},... | collective-permute-start | bytes 7688 | tf_op jit(solution)/shard_map/ppermute | solution.py:31
  177.0 5.2 %collective-permute-start.13 = (f32[5,32,1]{2,1,0:T(8,128)S(1)}, f32[5,32,1]{2,1,0:T(8,128)S(1)}, u32[]{:S(2)}, u32[]{:S(2)}) collective-permute-start(f32[5,32,1]{2,1,0:T(8,128)S(1)} %get-tuple-element.47), channel_id=1, source_target_pairs={{0,1},{1,0},{2,3},{3,2},{4,5},{5,4},{6,7},{7,6},{8,9},{9,8},{10,11... | collective-permute-start | bytes 1928 | tf_op jit(solution)/shard_map/ppermute | solution.py:28
  178.6 5.4 %collective-permute-start.12 = (f32[5,32,1]{2,1,0:T(8,128)S(1)}, f32[5,32,1]{2,1,0:T(8,128)S(1)}, u32[]{:S(2)}, u32[]{:S(2)}) collective-permute-start(f32[5,32,1]{2,1,0:T(8,128)S(1)} %get-tuple-element.46), channel_id=1, source_target_pairs={{1,0},{0,1},{3,2},{2,3},{5,4},{4,5},{7,6},{6,7},{9,8},{8,9},{11,10... | collective-permute-start | bytes 1928 | tf_op jit(solution)/shard_map/ppermute | solution.py:31
where the time goes:
time: 209 us; the launch traced here: 208 us
  blocking collectives  60 us (29%)
  other arithmetic  45.3 us (22%)
  local copies, waits for them, and re-layouts  38.1 us (18%)
  starting transfers between devices  35.1 us (17%)
  waiting for transfers between devices  26 us (12%)
  matrix products  2.11 us (1%)
    psum x2, blocking collectives, ocean_step(): divergence = lax.psum(partial_div, 'trc')  44.3 us
    mul x4, other arithmetic, face_flux(): return courant * jnp.where(courant >= 0, upwind_pos, upwind_neg)  18.3 us
    ppermute x8, waiting for transfers between devices, padded(): lax.ppermute(lax.slice_in_dim(block, block.shape[dim] - width, None, axis...  16.8 us
    all_gather x1, blocking collectives, body(): lax.all_gather(jnp.stack([east_start, north_start]), 'trc', axis=1, tiled...  15.7 us
    ppermute x8, starting transfers between devices, padded(): lax.ppermute(lax.slice_in_dim(block, block.shape[dim] - width, None, axis...  13.9 us
    ppermute x8, starting transfers between devices, padded(): lax.ppermute(lax.slice_in_dim(block, 0, width, axis=dim), axis, backward)  9.21 us
    ppermute x8, waiting for transfers between devices, padded(): lax.ppermute(lax.slice_in_dim(block, 0, width, axis=dim), axis, backward)  6.48 us
    concatenate x3, other arithmetic, padded(): block = jnp.concatenate([low, block, high], axis=dim)  6.44 us
  transfers between devices with their start and end apart: 19, of which 8 were waited for; matrix products, arithmetic and copies ran while one was open for 19% of the time, Pallas kernels for 0%

commit v1 on v0

--- a/solution.py
+++ b/solution.py
@@ -187,7 +187,16 @@
         zonal_flow_value, meridional_flow_value, free_top_height = ocean_step(
             zonal_flow_value, meridional_flow_value, free_top_height, wet_own, coriolis
         )
-    velocity = lax.all_gather(jnp.stack([east_start, north_start]), "trc", axis=1, tiled=True)
+    value = jnp.stack([east_start, north_start])
+    ways, here, step = (lax.axis_size("trc"), lax.axis_index("trc"), value.shape[1])
+    shape = [n * ways if d == 1 else n for d, n in enumerate(value.shape)]
+    full = lax.dynamic_update_slice_in_dim(
+        jnp.zeros(shape, value.dtype), value, here * step, axis=1
+    )
+    for far in range(1, ways):
+        value = lax.ppermute(value, "trc", [(d, (d + 1) % ways) for d in range(ways)])
+        full = lax.dynamic_update_slice_in_dim(full, value, (here - far) % ways * step, axis=1)
+    velocity = full
     flow = jnp.concatenate([velocity, wet_all[None]], 0)
     flow_ext = widen_flow(flow, 4)
     first = transport(

time: 209 us -> 213 us (1.019)
  blocking collectives: 60 us -> 44.4 us
  waiting for transfers between devices: 26 us -> 36.4 us
  starting transfers between devices: 35.1 us -> 39.6 us
  other arithmetic: 45.3 us -> 48.1 us
    all_gather x1 -> x0, blocking collectives: 15.7 us -> none  [body(): lax.all_gather(jnp.stack([east_start, north_start]), 'trc', axis=1, tiled...]
    ppermute x0 -> x3, starting transfers between devices: none -> 6.1 us  [body(): lax.ppermute(value, 'trc', [(d, (d + 1) % ways) for d in range(ways)])]
    ppermute x8, waiting for transfers between devices: 6.48 us -> 11.9 us  [padded(): lax.ppermute(lax.slice_in_dim(block, 0, width, axis=dim), axis, backward)]
    ppermute x0 -> x3, waiting for transfers between devices: none -> 4.92 us  [body(): lax.ppermute(value, 'trc', [(d, (d + 1) % ways) for d in range(ways)])]
    mul x4, other arithmetic: 18.3 us -> 22.6 us  [face_flux(): return courant * jnp.where(courant >= 0, upwind_pos, upwind_neg)]
    concatenate x3 -> x2, other arithmetic: 6.44 us -> 4.38 us  [padded(): block = jnp.concatenate([low, block, high], axis=dim)]
  transfers between devices with their start and end apart: 19 -> 22, of which waited for: 8 -> 11; matrix products, arithmetic and copies ran while one was open for 19% -> 11% of each run, Pallas kernels for 0% -> 0%
where the time goes in v1:
time: 213 us; the launch traced here: 212 us
  other arithmetic  48.1 us (23%)
  blocking collectives  44.4 us (21%)
  local copies, waits for them, and re-layouts  39.7 us (19%)
  starting transfers between devices  39.6 us (19%)
  waiting for transfers between devices  36.4 us (17%)
    psum x2, blocking collectives, ocean_step(): divergence = lax.psum(partial_div, 'trc')  44.4 us
    mul x4, other arithmetic, face_flux(): return courant * jnp.where(courant >= 0, upwind_pos, upwind_neg)  22.6 us
    ppermute x8, waiting for transfers between devices, padded(): lax.ppermute(lax.slice_in_dim(block, block.shape[dim] - width, None, axis...  16.9 us
    ppermute x8, starting transfers between devices, padded(): lax.ppermute(lax.slice_in_dim(block, block.shape[dim] - width, None, axis...  13.6 us
    ppermute x8, waiting for transfers between devices, padded(): lax.ppermute(lax.slice_in_dim(block, 0, width, axis=dim), axis, backward)  11.9 us
    ppermute x8, starting transfers between devices, padded(): lax.ppermute(lax.slice_in_dim(block, 0, width, axis=dim), axis, backward)  9.47 us
    mul x4, local copies, waits for them, and re-layouts, face_flux(): 0.5 * (1.0 - courant) * limited_slope(after - center, center - before)  7.62 us
    sub x2, other arithmetic, transport(): field[..., rows, cols] - (flux_x[..., 1:] - flux_x[..., :-1])  6.67 us
  transfers between devices with their start and end apart: 22, of which 11 were waited for; matrix products, arithmetic and copies ran while one was open for 11% of the time, Pallas kernels for 0%

profile of v1, /device:TPU:0, one launch (start us, length us, event | category | flops | bytes accessed | tf_op | source)
XLA Modules:
  0.0 211.7 jit_solution(5497111183337102706)
XLA Ops:
  3.1 3.0 %collective-permute-start = (f32[8,8,4,128]{3,1,2,0:T(8,128)S(1)}, f32[8,8,4,128]{3,1,2,0:T(8,128)S(1)}, u32[]{:S(2)}, u32[]{:S(2)}) collective-permute-start(f32[8,8,4,128]{3,1,2,0:T(8,128)S(1)} %copy.158), channel_id=1, source_target_pairs={{0,2},{2,4},{4,6},{1,3},{3,5},{5,7},{8,10},{10,12},{12,14},{9,11},... | collective-permute-start | bytes 393224 | tf_op jit(solution)/shard_map/ppermute | solution.py:28
  7.7 3.1 %collective-permute-start.4 = (f32[2,2,32,128]{3,2,1,0:T(8,128)S(1)}, f32[2,2,32,128]{3,2,1,0:T(8,128)S(1)}, u32[]{:S(2)}, u32[]{:S(2)}) collective-permute-start(f32[2,2,32,128]{3,2,1,0:T(8,128)S(1)} %get-tuple-element.51), channel_id=1, source_target_pairs={{0,8},{8,16},{16,24},{24,0},{1,9},{9,17},{17,25},{25,1},{2,10},{10... | collective-permute-start | bytes 196616 | tf_op jit(solution)/shard_map/ppermute | solution.py:197
  11.5 3.7 %copy.129 = f32[8,8,32,128]{2,1,3,0:T(8,128)} copy(f32[8,8,32,128]{3,2,1,0:T(8,128)} %param.9) | data formatting | bytes 2097152 | tf_op args[0]
  15.4 1.4 collective-permute-start.5
  16.8 2.7 %copy.130 = f32[8,8,4,128]{2,1,3,0:T(8,128)} copy(f32[8,8,4,128]{3,1,2,0:T(8,128)S(1)} %collective-permute-done.1) | data formatting | bytes 262144 | tf_op jit(solution)/shard_map/ppermute | solution.py:31
  19.5 2.8 %copy.128 = f32[8,8,4,128]{2,1,3,0:T(8,128)} copy(f32[8,8,4,128]{3,1,2,0:T(8,128)S(1)} %collective-permute-done) | data formatting | bytes 262144 | tf_op jit(solution)/shard_map/ppermute | solution.py:28
  22.3 1.6 collective-permute-start.6
  23.9 4.8 %collective-permute-done.6 = f32[2,2,32,128]{3,2,1,0:T(8,128)S(1)} collective-permute-done((f32[2,2,32,128]{3,2,1,0:T(8,128)S(1)}, f32[2,2,32,128]{3,2,1,0:T(8,128)S(1)}, u32[]{:S(2)}, u32[]{:S(2)}) %collective-permute-start.6) | collective-permute-done | bytes 65568 | tf_op jit(solution)/shard_map/ppermute | solution.py:197
  28.7 1.6 collective-permute-start.7
  30.3 1.6 pad_maximum_fusion.5
  31.9 1.6 collective-permute-start.3
  34.0 1.4 collective-permute-start.8
  35.7 2.3 %collective-permute-done.8 = f32[3,8,4,128]{3,1,2,0:T(8,128)S(1)} collective-permute-done((f32[3,8,4,128]{3,1,2,0:T(8,128)S(1)}, f32[3,8,4,128]{3,1,2,0:T(8,128)S(1)}, u32[]{:S(2)}, u32[]{:S(2)}) %collective-permute-start.8) | collective-permute-done | bytes 49184 | tf_op jit(solution)/shard_map/ppermute | solution.py:31
  38.2 1.6 collective-permute-start.10
  40.5 3.9 %pad_maximum_fusion = f32[8,8,40,136]{2,1,3,0:T(8,128)} fusion(f32[8,8,40,4]{2,1,3,0:T(8,128)S(1)} %collective-permute-done.3, f32[8,8,4,128]{2,1,3,0:T(8,128)S(1)} %copy-done.2, f32[8,8,32,128]{2,1,3,0:T(8,128)S(1)} %copy-done.1, f32[8,8,4,128]{2,1,3,0:T(8,128)S(1)} %copy-done.3, f32[8,8,40,4]{2,1,3,0:T(8,128)S(1)} %collective-permute-done.2), kind=kLoop, calls=%fused_computation.8 | loop fusion | flops 1392640 | bytes 2785280 | tf_op jit(solution)/shard_map/concatenate | solution.py:32
  44.4 6.1 %collective-permute-done.10 = f32[3,8,40,4]{3,1,2,0:T(8,128)S(1)} collective-permute-done((f32[3,8,40,4]{3,1,2,0:T(8,128)S(1)}, f32[3,8,40,4]{3,1,2,0:T(8,128)S(1)}, u32[]{:S(2)}, u32[]{:S(2)}) %collective-permute-start.10) | collective-permute-done | bytes 15392 | tf_op jit(solution)/shard_map/ppermute | solution.py:31
  50.5 10.5 %collective-permute-done.9 = f32[3,8,40,4]{3,1,2,0:T(8,128)S(1)} collective-permute-done((f32[3,8,40,4]{3,1,2,0:T(8,128)S(1)}, f32[3,8,40,4]{3,1,2,0:T(8,128)S(1)}, u32[]{:S(2)}, u32[]{:S(2)}) %collective-permute-start.9) | collective-permute-done | bytes 15392 | tf_op jit(solution)/shard_map/ppermute | solution.py:28
  71.5 1.4 copy.141
  72.9 2.1 %copy.140 = f32[8,37,132]{1,0,2:T(8,128)} copy(f32[8,37,132]{2,0,1:T(8,128)} %get-tuple-element.27) | data formatting | bytes 312576 | tf_op jit(solution)/shard_map/mul | solution.py:45
  76.1 1.4 copy.137
  77.5 1.4 copy.136
  78.8 1.3 copy.135
  80.2 1.9 copy.149
  82.1 2.0 copy.148
  84.1 1.7 copy.147
  86.9 2.2 %copy.144 = f32[8,32,129]{1,0,2:T(8,128)} copy(f32[8,32,129]{2,0,1:T(8,128)} %get-tuple-element.31) | data formatting | bytes 264192 | tf_op jit(solution)/shard_map/mul | solution.py:45
  90.1 8.8 %fusion.12 = f32[8,8,37,132]{2,1,3,0:T(8,128)S(1)} fusion(f32[8,8,40,136]{2,1,3,0:T(8,128)} %pad_maximum_fusion, f32[8,37,132]{1,0,2:T(8,128)S(1)} %copy.141, f32[8,37,132]{1,0,2:T(8,128)} %copy.140, f32[8,37,132]{1,0,2:T(8,128)S(1)} %copy.138, pred[8,37,132]{1,0,2:T(8,128)(4,1)} %copy.139), kind=kLoop, calls=%fused_computation.26 | loop fusion | flops 8126976 | bytes 6759456 | tf_op jit(solution)/shard_map/mul | solution.py:47
  98.9 4.9 %fusion.4 = f32[8,8,36,133]{2,1,3,0:T(8,128)S(1)} fusion(f32[8,8,40,136]{2,1,3,0:T(8,128)S(1)} %bitcast.68, f32[8,36,133]{1,0,2:T(8,128)S(1)} %copy.137, f32[8,36,133]{1,0,2:T(8,128)S(1)} %copy.136, f32[8,36,133]{1,0,2:T(8,128)S(1)} %copy.134, pred[8,36,133]{1,0,2:T(8,128)(4,1)S(1)} %copy.135), kind=kLoop, calls=%fused_computation.13 | loop fusion | flops 7967232 | bytes 6626592 | tf_op jit(solution)/shard_map/mul | solution.py:47
  103.9 2.9 %fusion.16 = f32[8,8,36,132]{2,1,3,0:T(8,128)S(1)} fusion(f32[8,8,37,132]{2,1,3,0:T(8,128)S(1)} %fusion.12, f32[8,8,36,133]{2,1,3,0:T(8,128)S(1)} %fusion.4, f32[8,8,40,136]{2,1,3,0:T(8,128)S(1)} %bitcast.68), kind=kLoop, calls=%fused_computation.31 | loop fusion | flops 1216512 | bytes 7299072 | tf_op jit(solution)/shard_map/sub | solution.py:75
  106.8 4.2 %fusion.30 = f32[8,8,33,128]{2,1,3,0:T(8,128)S(1)} fusion(f32[8,8,36,132]{2,1,3,0:T(8,128)S(1)} %fusion.16, f32[8,33,128]{1,0,2:T(8,128)S(1)} %copy-done.8, f32[8,33,128]{1,0,2:T(8,128)S(1)} %copy-done.9, f32[8,33,128]{1,0,2:T(8,128)S(1)} %copy-done.7, pred[8,33,128]{1,0,2:T(8,128)(4,1)S(1)} %copy-done.13), kind=kLoop, calls=%fused_computation.56 | loop fusion | flops 7028736 | bytes 5846016 | tf_op jit(solution)/shard_map/mul | solution.py:47
  111.1 4.7 %fusion.22 = f32[8,8,32,129]{2,1,3,0:T(8,128)S(1)} fusion(f32[8,8,36,132]{2,1,3,0:T(8,128)S(1)} %fusion.16, f32[8,32,129]{1,0,2:T(8,128)S(1)} %copy-done.5, f32[8,32,129]{1,0,2:T(8,128)S(1)} %copy-done.6, f32[8,32,129]{1,0,2:T(8,128)S(1)} %copy-done.4, pred[8,32,129]{1,0,2:T(8,128)(4,1)S(1)} %copy-done.12), kind=kLoop, calls=%fused_computation.43 | loop fusion | flops 6868992 | bytes 5713152 | tf_op jit(solution)/shard_map/mul | solution.py:47
  115.8 3.8 %fusion.34 = f32[8,8,32,128]{2,1,3,0:T(8,128)} fusion(f32[8,8,33,128]{2,1,3,0:T(8,128)S(1)} %fusion.30, f32[8,8,32,129]{2,1,3,0:T(8,128)S(1)} %fusion.22, f32[8,8,36,132]{2,1,3,0:T(8,128)S(1)} %fusion.16), kind=kLoop, calls=%fused_computation.61 | loop fusion | flops 1048576 | bytes 6291456 | tf_op jit(solution)/shard_map/sub | solution.py:75
  119.6 3.9 %copy.150 = f32[8,8,32,128]{3,1,0,2:T(8,128)} copy(f32[8,8,32,128]{2,1,3,0:T(8,128)} %fusion.34) | data formatting | bytes 2097152 | tf_op jit(solution)/shard_map/sub | solution.py:75
  123.6 3.5 %all-to-all-start = ((f32[8,8,32,128]{3,1,0,2:T(8,128)}), f32[8,8,32,128]{3,1,0,2:T(8,128)S(1)}, u32[]{:S(2)}, u32[]{:S(2)}) async-start(f32[8,8,32,128]{3,1,0,2:T(8,128)} %copy.150), calls=%async_computation | async-start | bytes 2097152 | tf_op jit(solution)/shard_map/all_to_all | solution.py:208
  127.1 3.5 %collective-permute-start.14 = (f32[5,1,128]{2,1,0:T(1,128)S(1)}, f32[5,1,128]{2,1,0:T(1,128)S(1)}, u32[]{:S(2)}, u32[]{:S(2)}) collective-permute-start(f32[5,1,128]{2,1,0:T(1,128)S(1)} %get-tuple-element.50), channel_id=1, source_target_pairs={{0,2},{2,4},{4,6},{1,3},{3,5},{5,7},{8,10},{10,12},{12,14},{9,11},... | collective-permute-start | bytes 7688 | tf_op jit(solution)/shard_map/ppermute | solution.py:28
  132.1 1.6 collective-permute-start.12
  134.3 3.0 %collective-permute-done.12 = f32[5,32,1]{2,1,0:T(8,128)S(1)} collective-permute-done((f32[5,32,1]{2,1,0:T(8,128)S(1)}, f32[5,32,1]{2,1,0:T(8,128)S(1)}, u32[]{:S(2)}, u32[]{:S(2)}) %collective-permute-start.12) | collective-permute-done | bytes 672 | tf_op jit(solution)/shard_map/ppermute | solution.py:28
  137.3 1.8 collective-permute-done.11
  139.2 22.9 %psum.14 = f32[32,128]{1,0:T(8,128)S(1)} all-reduce(f32[32,128]{1,0:T(8,128)S(1)} %multiply_reduce_fusion.1), channel_id=1, replica_groups=mesh['trc'=4,'lat'=4,'lon'=2] {'trc'}, use_global_device_ids=true, to_apply=%region_2.0 | all-reduce | flops 4096 | bytes 32768 | tf_op jit(solution)/shard_map/psum | solution.py:135
  163.9 3.4 %all-to-all-start.2 = ((f32[8,8,128]{2,1,0:T(8,128)}), f32[8,8,128]{2,1,0:T(8,128)S(1)}, u32[]{:S(2)}, u32[]{:S(2)}) async-start(f32[8,8,128]{2,1,0:T(8,128)} %get-tuple-element.35), calls=%async_computation.2 | async-start | bytes 65536 | tf_op jit(solution)/shard_map/all_to_all | solution.py:220
  167.3 1.3 fusion.38
  168.6 1.6 copy.152
  170.2 2.7 %all-to-all-done.2 = f32[8,8,128]{2,1,0:T(8,128)S(1)} async-done(((f32[8,8,128]{2,1,0:T(8,128)}), f32[8,8,128]{2,1,0:T(8,128)S(1)}, u32[]{:S(2)}, u32[]{:S(2)}) %all-to-all-start.2) | async-done | bytes 32800 | tf_op jit(solution)/shard_map/all_to_all | solution.py:220
  172.9 3.5 %all-to-all-start.1 = ((f32[32,8,8,128]{3,2,1,0:T(8,128)}), f32[32,8,8,128]{3,2,1,0:T(8,128)S(1)}, u32[]{:S(2)}, u32[]{:S(2)}) async-start(f32[32,8,8,128]{3,2,1,0:T(8,128)} %copy.152), calls=%async_computation.1 | async-start | bytes 2097152 | tf_op jit(solution)/shard_map/all_to_all | solution.py:217
  179.2 1.6 collective-permute-start.16
  181.2 3.1 %collective-permute-done.16 = f32[5,32,1]{2,1,0:T(8,128)S(1)} collective-permute-done((f32[5,32,1]{2,1,0:T(8,128)S(1)}, f32[5,32,1]{2,1,0:T(8,128)S(1)}, u32[]{:S(2)}, u32[]{:S(2)}) %collective-permute-start.16) | collective-permute-done | bytes 672 | tf_op jit(solution)/shard_map/ppermute | solution.py:28
  184.4 1.8 collective-permute-done.15
  186.2 21.6 %psum.15 = f32[32,128]{1,0:T(8,128)S(1)} all-reduce(f32[32,128]{1,0:T(8,128)S(1)} %multiply_reduce_fusion), channel_id=1, replica_groups=mesh['trc'=4,'lat'=4,'lon'=2] {'trc'}, use_global_device_ids=true, to_apply=%region_4.5 | all-reduce | flops 4096 | bytes 32768 | tf_op jit(solution)/shard_map/psum | solution.py:135
  (122 shorter events, 31.5 us)
Async XLA Ops:
  0.6 166.6 %copy-start = (f32[32,32]{1,0:T(8,128)S(1)}, f32[32,32]{1,0:T(8,128)}, u32[]{:S(2)}) copy-start(f32[32,32]{1,0:T(8,128)} %param.15) | copy-start | bytes 12292
  1.8 15.0 %collective-permute-start.1 = (f32[8,8,4,128]{3,1,2,0:T(8,128)S(1)}, f32[8,8,4,128]{3,1,2,0:T(8,128)S(1)}, u32[]{:S(2)}, u32[]{:S(2)}) collective-permute-start(f32[8,8,4,128]{3,1,2,0:T(8,128)S(1)} %copy.159), channel_id=1, source_target_pairs={{2,0},{4,2},{6,4},{3,1},{5,3},{7,5},{10,8},{12,10},{14,12},{11,9},... | collective-permute-start | bytes 393224 | tf_op jit(solution)/shard_map/ppermute | solution.py:31
  3.1 16.4 %collective-permute-start = (f32[8,8,4,128]{3,1,2,0:T(8,128)S(1)}, f32[8,8,4,128]{3,1,2,0:T(8,128)S(1)}, u32[]{:S(2)}, u32[]{:S(2)}) collective-permute-start(f32[8,8,4,128]{3,1,2,0:T(8,128)S(1)} %copy.158), channel_id=1, source_target_pairs={{0,2},{2,4},{4,6},{1,3},{3,5},{5,7},{8,10},{10,12},{12,14},{9,11},... | collective-permute-start | bytes 393224 | tf_op jit(solution)/shard_map/ppermute | solution.py:28
  7.7 7.7 %collective-permute-start.4 = (f32[2,2,32,128]{3,2,1,0:T(8,128)S(1)}, f32[2,2,32,128]{3,2,1,0:T(8,128)S(1)}, u32[]{:S(2)}, u32[]{:S(2)}) collective-permute-start(f32[2,2,32,128]{3,2,1,0:T(8,128)S(1)} %get-tuple-element.51), channel_id=1, source_target_pairs={{0,8},{8,16},{16,24},{24,0},{1,9},{9,17},{17,25},{25,1},{2,10},{10... | collective-permute-start | bytes 196616 | tf_op jit(solution)/shard_map/ppermute | solution.py:197
  15.4 6.9 %collective-permute-start.5 = (f32[2,2,32,128]{3,2,1,0:T(8,128)S(1)}, f32[2,2,32,128]{3,2,1,0:T(8,128)S(1)}, u32[]{:S(2)}, u32[]{:S(2)}) collective-permute-start(f32[2,2,32,128]{3,2,1,0:T(8,128)S(1)} %collective-permute-done.4), channel_id=1, source_target_pairs={{0,8},{8,16},{16,24},{24,0},{1,9},{9,17},{17,25},{25,1},{2,10},{10... | collective-permute-start | bytes 196616 | tf_op jit(solution)/shard_map/ppermute | solution.py:197
  22.3 6.3 %collective-permute-start.6 = (f32[2,2,32,128]{3,2,1,0:T(8,128)S(1)}, f32[2,2,32,128]{3,2,1,0:T(8,128)S(1)}, u32[]{:S(2)}, u32[]{:S(2)}) collective-permute-start(f32[2,2,32,128]{3,2,1,0:T(8,128)S(1)} %collective-permute-done.5), channel_id=1, source_target_pairs={{0,8},{8,16},{16,24},{24,0},{1,9},{9,17},{17,25},{25,1},{2,10},{10... | collective-permute-start | bytes 196616 | tf_op jit(solution)/shard_map/ppermute | solution.py:197
  28.7 6.7 %collective-permute-start.7 = (f32[3,8,4,128]{3,1,2,0:T(8,128)S(1)}, f32[3,8,4,128]{3,1,2,0:T(8,128)S(1)}, u32[]{:S(2)}, u32[]{:S(2)}) collective-permute-start(f32[3,8,4,128]{3,1,2,0:T(8,128)S(1)} %copy.171), channel_id=1, source_target_pairs={{0,2},{2,4},{4,6},{1,3},{3,5},{5,7},{8,10},{10,12},{12,14},{9,11},... | collective-permute-start | bytes 147464 | tf_op jit(solution)/shard_map/ppermute | solution.py:28
  30.3 10.2 %copy-start.1 = (f32[8,8,32,128]{2,1,3,0:T(8,128)S(1)}, f32[8,8,32,128]{2,1,3,0:T(8,128)}, u32[]{:S(2)}) copy-start(f32[8,8,32,128]{2,1,3,0:T(8,128)} %copy.129) | copy-start | bytes 3145732
  30.3 10.2 %copy-start.2 = (f32[8,8,4,128]{2,1,3,0:T(8,128)S(1)}, f32[8,8,4,128]{2,1,3,0:T(8,128)}, u32[]{:S(2)}) copy-start(f32[8,8,4,128]{2,1,3,0:T(8,128)} %copy.130) | copy-start | bytes 393220
  30.3 10.2 %copy-start.3 = (f32[8,8,4,128]{2,1,3,0:T(8,128)S(1)}, f32[8,8,4,128]{2,1,3,0:T(8,128)}, u32[]{:S(2)}) copy-start(f32[8,8,4,128]{2,1,3,0:T(8,128)} %copy.128) | copy-start | bytes 393220
  31.9 8.3 %collective-permute-start.3 = (f32[8,8,40,4]{2,1,3,0:T(8,128)S(1)}, f32[8,8,40,4]{2,1,3,0:T(8,128)S(1)}, u32[]{:S(2)}, u32[]{:S(2)}) collective-permute-start(f32[8,8,40,4]{2,1,3,0:T(8,128)S(1)} %get-tuple-element.14), channel_id=1, source_target_pairs={{1,0},{0,1},{3,2},{2,3},{5,4},{4,5},{7,6},{6,7},{9,8},{8,9},{11,10... | collective-permute-start | bytes 122888 | tf_op jit(solution)/shard_map/ppermute | solution.py:31
  33.5 7.0 %collective-permute-start.2 = (f32[8,8,40,4]{2,1,3,0:T(8,128)S(1)}, f32[8,8,40,4]{2,1,3,0:T(8,128)S(1)}, u32[]{:S(2)}, u32[]{:S(2)}) collective-permute-start(f32[8,8,40,4]{2,1,3,0:T(8,128)S(1)} %get-tuple-element.13), channel_id=1, source_target_pairs={{0,1},{1,0},{2,3},{3,2},{4,5},{5,4},{6,7},{7,6},{8,9},{9,8},{10,11... | collective-permute-start | bytes 122888 | tf_op jit(solution)/shard_map/ppermute | solution.py:28
  34.0 4.0 %collective-permute-start.8 = (f32[3,8,4,128]{3,1,2,0:T(8,128)S(1)}, f32[3,8,4,128]{3,1,2,0:T(8,128)S(1)}, u32[]{:S(2)}, u32[]{:S(2)}) collective-permute-start(f32[3,8,4,128]{3,1,2,0:T(8,128)S(1)} %copy.172), channel_id=1, source_target_pairs={{2,0},{4,2},{6,4},{3,1},{5,3},{7,5},{10,8},{12,10},{14,12},{11,9},... | collective-permute-start | bytes 147464 | tf_op jit(solution)/shard_map/ppermute | solution.py:31
  38.2 12.3 %collective-permute-start.10 = (f32[3,8,40,4]{3,1,2,0:T(8,128)S(1)}, f32[3,8,40,4]{3,1,2,0:T(8,128)S(1)}, u32[]{:S(2)}, u32[]{:S(2)}) collective-permute-start(f32[3,8,40,4]{3,1,2,0:T(8,128)S(1)} %get-tuple-element.24), channel_id=1, source_target_pairs={{1,0},{0,1},{3,2},{2,3},{5,4},{4,5},{7,6},{6,7},{9,8},{8,9},{11,10... | collective-permute-start | bytes 46088 | tf_op jit(solution)/shard_map/ppermute | solution.py:31
  39.7 21.3 %collective-permute-start.9 = (f32[3,8,40,4]{3,1,2,0:T(8,128)S(1)}, f32[3,8,40,4]{3,1,2,0:T(8,128)S(1)}, u32[]{:S(2)}, u32[]{:S(2)}) collective-permute-start(f32[3,8,40,4]{3,1,2,0:T(8,128)S(1)} %get-tuple-element.23), channel_id=1, source_target_pairs={{0,1},{1,0},{2,3},{3,2},{4,5},{5,4},{6,7},{7,6},{8,9},{9,8},{10,11... | collective-permute-start | bytes 46088 | tf_op jit(solution)/shard_map/ppermute | solution.py:28
  69.4 19.6 %copy-start.14 = (pred[8,32,129]{2,0,1:T(8,128)(4,1)S(1)}, pred[8,32,129]{2,0,1:T(8,128)(4,1)}, u32[]{:S(2)}) copy-start(pred[8,32,129]{2,0,1:T(8,128)(4,1)} %get-tuple-element.5) | copy-start | bytes 99076
  71.5 14.2 %copy-start.10 = (f32[8,32,129]{2,0,1:T(8,128)S(1)}, f32[8,32,129]{2,0,1:T(8,128)}, u32[]{:S(2)}) copy-start(f32[8,32,129]{2,0,1:T(8,128)} %get-tuple-element.32) | copy-start | bytes 396292
  86.9 12.0 %slice-start = ((s8[4456448]{0:T(1024)(128)(4,1)}), s8[262144]{0:T(1024)(128)(4,1)S(1)}, s32[]{:S(2)}) async-start(s8[4456448]{0:T(1024)(128)(4,1)} %bitcast.67), calls=%async_computation.3 | async-start | bytes 524288
  90.1 8.8 %slice-start.1 = ((s8[4456448]{0:T(1024)(128)(4,1)}), s8[4194304]{0:T(1024)(128)(4,1)S(1)}, s32[]{:S(2)}) async-start(s8[4456448]{0:T(1024)(128)(4,1)} %bitcast.67), calls=%async_computation.4 | async-start | bytes 8388608
  103.8 2.9 %copy-start.7 = (f32[8,33,128]{1,0,2:T(8,128)S(1)}, f32[8,33,128]{1,0,2:T(8,128)}, u32[]{:S(2)}) copy-start(f32[8,33,128]{1,0,2:T(8,128)} %copy.146) | copy-start | bytes 405508
  103.8 2.9 %copy-start.8 = (f32[8,33,128]{1,0,2:T(8,128)S(1)}, f32[8,33,128]{1,0,2:T(8,128)}, u32[]{:S(2)}) copy-start(f32[8,33,128]{1,0,2:T(8,128)} %copy.149) | copy-start | bytes 405508
  103.8 2.9 %copy-start.9 = (f32[8,33,128]{1,0,2:T(8,128)S(1)}, f32[8,33,128]{1,0,2:T(8,128)}, u32[]{:S(2)}) copy-start(f32[8,33,128]{1,0,2:T(8,128)} %copy.148) | copy-start | bytes 405508
  103.9 2.9 %copy-start.13 = (pred[8,33,128]{1,0,2:T(8,128)(4,1)S(1)}, pred[8,33,128]{1,0,2:T(8,128)(4,1)}, u32[]{:S(2)}) copy-start(pred[8,33,128]{1,0,2:T(8,128)(4,1)} %copy.147) | copy-start | bytes 101380
  106.8 4.3 %copy-start.4 = (f32[8,32,129]{1,0,2:T(8,128)S(1)}, f32[8,32,129]{1,0,2:T(8,128)}, u32[]{:S(2)}) copy-start(f32[8,32,129]{1,0,2:T(8,128)} %copy.142) | copy-start | bytes 396292
  106.8 4.3 %copy-start.5 = (f32[8,32,129]{1,0,2:T(8,128)S(1)}, f32[8,32,129]{1,0,2:T(8,128)}, u32[]{:S(2)}) copy-start(f32[8,32,129]{1,0,2:T(8,128)} %copy.145) | copy-start | bytes 396292
  106.8 4.3 %copy-start.6 = (f32[8,32,129]{1,0,2:T(8,128)S(1)}, f32[8,32,129]{1,0,2:T(8,128)}, u32[]{:S(2)}) copy-start(f32[8,32,129]{1,0,2:T(8,128)} %copy.144) | copy-start | bytes 396292
  106.8 4.3 %copy-start.12 = (pred[8,32,129]{1,0,2:T(8,128)(4,1)S(1)}, pred[8,32,129]{1,0,2:T(8,128)(4,1)}, u32[]{:S(2)}) copy-start(pred[8,32,129]{1,0,2:T(8,128)(4,1)} %copy.143) | copy-start | bytes 99076
  119.6 7.5 %copy-start.11 = (f32[32,128]{1,0:T(8,128)S(1)}, f32[32,128]{1,0:T(8,128)}, u32[]{:S(2)}) copy-start(f32[32,128]{1,0:T(8,128)} %param.13) | copy-start | bytes 49156
  119.6 42.8 %copy-start.16 = (f32[32]{0:T(128)S(1)}, f32[32]{0:T(128)}, u32[]{:S(2)}) copy-start(f32[32]{0:T(128)} %param.17) | copy-start | bytes 388
  119.6 47.7 %copy-start.17 = (f32[32]{0:T(128)S(1)}, f32[32]{0:T(128)}, u32[]{:S(2)}) copy-start(f32[32]{0:T(128)} %param.16) | copy-start | bytes 388
  123.6 38.8 %all-to-all-start = ((f32[8,8,32,128]{3,1,0,2:T(8,128)}), f32[8,8,32,128]{3,1,0,2:T(8,128)S(1)}, u32[]{:S(2)}, u32[]{:S(2)}) async-start(f32[8,8,32,128]{3,1,0,2:T(8,128)} %copy.150), calls=%async_computation | async-start | bytes 2097152 | tf_op jit(solution)/shard_map/all_to_all | solution.py:208
  127.1 11.9 %collective-permute-start.14 = (f32[5,1,128]{2,1,0:T(1,128)S(1)}, f32[5,1,128]{2,1,0:T(1,128)S(1)}, u32[]{:S(2)}, u32[]{:S(2)}) collective-permute-start(f32[5,1,128]{2,1,0:T(1,128)S(1)} %get-tuple-element.50), channel_id=1, source_target_pairs={{0,2},{2,4},{4,6},{1,3},{3,5},{5,7},{8,10},{10,12},{12,14},{9,11},... | collective-permute-start | bytes 7688 | tf_op jit(solution)/shard_map/ppermute | solution.py:28
  130.7 8.4 %collective-permute-start.13 = (f32[5,1,128]{2,1,0:T(1,128)S(1)}, f32[5,1,128]{2,1,0:T(1,128)S(1)}, u32[]{:S(2)}, u32[]{:S(2)}) collective-permute-start(f32[5,1,128]{2,1,0:T(1,128)S(1)} %get-tuple-element.49), channel_id=1, source_target_pairs={{2,0},{4,2},{6,4},{3,1},{5,3},{7,5},{10,8},{12,10},{14,12},{11,9},... | collective-permute-start | bytes 7688 | tf_op jit(solution)/shard_map/ppermute | solution.py:31
  132.1 5.2 %collective-permute-start.12 = (f32[5,32,1]{2,1,0:T(8,128)S(1)}, f32[5,32,1]{2,1,0:T(8,128)S(1)}, u32[]{:S(2)}, u32[]{:S(2)}) collective-permute-start(f32[5,32,1]{2,1,0:T(8,128)S(1)} %get-tuple-element.48), channel_id=1, source_target_pairs={{0,1},{1,0},{2,3},{3,2},{4,5},{5,4},{6,7},{7,6},{8,9},{9,8},{10,11... | collective-permute-start | bytes 1928 | tf_op jit(solution)/shard_map/ppermute | solution.py:28
  133.6 5.4 %collective-permute-start.11 = (f32[5,32,1]{2,1,0:T(8,128)S(1)}, f32[5,32,1]{2,1,0:T(8,128)S(1)}, u32[]{:S(2)}, u32[]{:S(2)}) collective-permute-start(f32[5,32,1]{2,1,0:T(8,128)S(1)} %get-tuple-element.47), channel_id=1, source_target_pairs={{1,0},{0,1},{3,2},{2,3},{5,4},{4,5},{7,6},{6,7},{9,8},{8,9},{11,10... | collective-permute-start | bytes 1928 | tf_op jit(solution)/shard_map/ppermute | solution.py:31
  163.9 46.1 %copy-start.15 = (f32[2,32,128]{2,1,0:T(8,128)S(1)}, f32[2,32,128]{2,1,0:T(8,128)}, u32[]{:S(2)}) copy-start(f32[2,32,128]{2,1,0:T(8,128)} %param.12) | copy-start | bytes 98308
  163.9 9.0 %all-to-all-start.2 = ((f32[8,8,128]{2,1,0:T(8,128)}), f32[8,8,128]{2,1,0:T(8,128)S(1)}, u32[]{:S(2)}, u32[]{:S(2)}) async-start(f32[8,8,128]{2,1,0:T(8,128)} %get-tuple-element.35), calls=%async_computation.2 | async-start | bytes 65536 | tf_op jit(solution)/shard_map/all_to_all | solution.py:220
  172.9 37.7 %all-to-all-start.1 = ((f32[32,8,8,128]{3,2,1,0:T(8,128)}), f32[32,8,8,128]{3,2,1,0:T(8,128)S(1)}, u32[]{:S(2)}, u32[]{:S(2)}) async-start(f32[32,8,8,128]{3,2,1,0:T(8,128)} %copy.152), calls=%async_computation.1 | async-start | bytes 2097152 | tf_op jit(solution)/shard_map/all_to_all | solution.py:217
  176.5 9.7 %collective-permute-start.18 = (f32[5,1,128]{2,1,0:T(1,128)S(1)}, f32[5,1,128]{2,1,0:T(1,128)S(1)}, u32[]{:S(2)}, u32[]{:S(2)}) collective-permute-start(f32[5,1,128]{2,1,0:T(1,128)S(1)} %get-tuple-element.44), channel_id=1, source_target_pairs={{0,2},{2,4},{4,6},{1,3},{3,5},{5,7},{8,10},{10,12},{12,14},{9,11},... | collective-permute-start | bytes 7688 | tf_op jit(solution)/shard_map/ppermute | solution.py:28
  177.7 8.4 %collective-permute-start.17 = (f32[5,1,128]{2,1,0:T(1,128)S(1)}, f32[5,1,128]{2,1,0:T(1,128)S(1)}, u32[]{:S(2)}, u32[]{:S(2)}) collective-permute-start(f32[5,1,128]{2,1,0:T(1,128)S(1)} %get-tuple-element.43), channel_id=1, source_target_pairs={{2,0},{4,2},{6,4},{3,1},{5,3},{7,5},{10,8},{12,10},{14,12},{11,9},... | collective-permute-start | bytes 7688 | tf_op jit(solution)/shard_map/ppermute | solution.py:31
  179.2 5.2 %collective-permute-start.16 = (f32[5,32,1]{2,1,0:T(8,128)S(1)}, f32[5,32,1]{2,1,0:T(8,128)S(1)}, u32[]{:S(2)}, u32[]{:S(2)}) collective-permute-start(f32[5,32,1]{2,1,0:T(8,128)S(1)} %get-tuple-element.42), channel_id=1, source_target_pairs={{0,1},{1,0},{2,3},{3,2},{4,5},{5,4},{6,7},{7,6},{8,9},{9,8},{10,11... | collective-permute-start | bytes 1928 | tf_op jit(solution)/shard_map/ppermute | solution.py:28
  180.7 5.4 %collective-permute-start.15 = (f32[5,32,1]{2,1,0:T(8,128)S(1)}, f32[5,32,1]{2,1,0:T(8,128)S(1)}, u32[]{:S(2)}, u32[]{:S(2)}) collective-permute-start(f32[5,32,1]{2,1,0:T(8,128)S(1)} %get-tuple-element.41), channel_id=1, source_target_pairs={{1,0},{0,1},{3,2},{2,3},{5,4},{4,5},{7,6},{6,7},{9,8},{8,9},{11,10... | collective-permute-start | bytes 1928 | tf_op jit(solution)/shard_map/ppermute | solution.py:31
